TPU v7x, 32 devices: a whole 2x2x4 slice. The times are simulated.
32 devices in a mesh: shard: 4 (over y, x), ctx: 2 (over core), tp: 4 (over z).
Axes of the slice: x: 2, y: 2, z: 4, core: 2. Of those that a mesh axis runs over, the one named last changes fastest.
Arguments:
- tokens: bfloat16 [4, 1024, 1536], P('shard', ('ctx', 'tp')), may hold values from -6 to 6
- cotangent: bfloat16 [4, 1024, 1536], P('shard', ('ctx', 'tp')), may hold values from -6 to 6
- lengths: int32 [4], P('shard'), may hold values from 256 to 1024, as said below
- w_qkv: bfloat16 [1536, 3, 1536], P(('shard', 'ctx'), None, 'tp'), may hold values from -0.15625 to 0.15625
- w_forget: bfloat16 [1536, 24], P(('shard', 'ctx'), 'tp'), may hold values from -0.15625 to 0.15625
- forget_bias: float32 [24], replicated, may hold values from 3 to 8
- w_ogate: bfloat16 [1536, 1536], P(('shard', 'ctx'), 'tp'), may hold values from -0.15625 to 0.15625
- w_out: bfloat16 [1536, 1536], P(('shard', 'ctx'), 'tp'), may hold values from -0.625 to 0.625
- w_gu: bfloat16 [1536, 2, 4096], P(('shard', 'ctx'), None, 'tp'), may hold values from -0.15625 to 0.15625
- w_down: bfloat16 [1536, 4096], P(('shard', 'ctx'), 'tp'), may hold values from -0.09375 to 0.09375
- gain_attn: float32 [1536], replicated, may hold values from 0.5 to 1.5
- gain_mlp: float32 [1536], replicated, may hold values from 0.5 to 1.5
- qk_gain: float32 [2, 64], replicated, may hold values from 1 to 2
Outputs:
- output: bfloat16 [4, 1024, 1536], P('shard', ('ctx', 'tp'))
- input_grad: bfloat16 [4, 1024, 1536], P('shard', ('ctx', 'tp'))
- grad_qkv: float32 [1536, 3, 1536], P(('shard', 'ctx'), None, 'tp')
- grad_forget: float32 [1536, 24], P(('shard', 'ctx'), 'tp')
- grad_forget_bias: float32 [24], replicated
- grad_ogate: float32 [1536, 1536], P(('shard', 'ctx'), 'tp')
- grad_out: float32 [1536, 1536], P(('shard', 'ctx'), 'tp')
- grad_gu: float32 [1536, 2, 4096], P(('shard', 'ctx'), None, 'tp')
- grad_down: float32 [1536, 4096], P(('shard', 'ctx'), 'tp')
- grad_gain_attn: float32 [1536], replicated
- grad_gain_mlp: float32 [1536], replicated
- grad_qk_gain: float32 [2, 64], replicated
Inputs may be any that keep to these rules, and one draw needn't show every extreme that they name: `lengths`: real tokens of a slot; positions at or past it are padding; both the least and the most value occur in every draw.
All inputs are finite; a program needn't handle non-finite values.
Results may differ from a plain program's by a relative error of at most 0.04.
Values may be sent and summed in bfloat16 or wider, within the bound.
No kernel may reach another device: no remote copies, remote signals or barrier semaphores. Data moves between devices by JAX's collectives and lax.ppermute only.
A program may use at most 128 MiB of HBM per device.

v0:
```python
import math
import jax
import jax.numpy as jnp
from jax import lax
from jax.sharding import PartitionSpec as P

epsilon = 1e-06


def shifted(block, axis, distance):
    devices = range(lax.axis_size(axis))
    route = [(i - distance, i) for i in devices if i - distance in devices]
    return lax.ppermute(block, axis, route)


def norm_rows(values, gain):
    return values * lax.rsqrt(jnp.mean(values * values, axis=-1, keepdims=True) + epsilon) * gain


def product(left, right):
    return jnp.dot(left, right, preferred_element_type=jnp.float32)


def product_t(left, right):
    return lax.dot_general(
        left, right, (((1,), (1,)), ((), ())), preferred_element_type=jnp.float32
    )


def outer_rows(left, right):
    return lax.dot_general(
        left, right, (((0,), (0,)), ((), ())), preferred_element_type=jnp.float32
    )


def body(
    tokens,
    cotangent,
    lengths,
    w_qkv,
    w_forget,
    forget_bias,
    w_ogate,
    w_out,
    w_gu,
    w_down,
    gain_attn,
    gain_mlp,
    qk_gain,
):
    slot_count, own_rows, model_width = tokens.shape
    tensor_size = lax.axis_size("tp")
    tensor_place = lax.axis_index("tp")
    span_index = lax.axis_index("ctx")
    half_rows = own_rows * tensor_size
    row_count = slot_count * half_rows
    local_heads = w_forget.shape[1]
    head_size = qk_gain.shape[1]
    head_cols = local_heads * head_size
    hidden_units = w_down.shape[1]
    item_count = slot_count * local_heads
    score_scale = 1.0 / math.sqrt(head_size)
    own_start = tensor_place * own_rows
    full_tokens, full_cot = (
        lax.all_gather(tokens, "tp", axis=1, tiled=True),
        lax.all_gather(cotangent, "tp", axis=1, tiled=True),
    )
    qkv_full, forget_full, ogate_full, out_full, gu_full, down_full = (
        lax.all_gather(w_qkv, ("shard", "ctx"), axis=0, tiled=True),
        lax.all_gather(w_forget, ("shard", "ctx"), axis=0, tiled=True),
        lax.all_gather(w_ogate, ("shard", "ctx"), axis=0, tiled=True),
        lax.all_gather(w_out, ("shard", "ctx"), axis=0, tiled=True),
        lax.all_gather(w_gu, ("shard", "ctx"), axis=0, tiled=True),
        lax.all_gather(w_down, ("shard", "ctx"), axis=0, tiled=True),
    )
    qkv_flat = qkv_full.reshape(model_width, 3 * head_cols)
    gu_flat = gu_full.reshape(model_width, 2 * hidden_units)

    def own_slice(values):
        return lax.dynamic_slice_in_dim(
            values.reshape(slot_count, half_rows, values.shape[-1]), own_start, own_rows, 1
        )

    positions = span_index * half_rows + jnp.arange(half_rows, dtype=jnp.int32)
    valid_rows = (positions[None, :] < lengths[:, None]).astype(jnp.float32).reshape(row_count, 1)
    own_positions = span_index * half_rows + own_start + jnp.arange(own_rows, dtype=jnp.int32)
    valid_own = (own_positions[None, :] < lengths[:, None]).astype(jnp.float32)[:, :, None]
    residual = full_tokens.reshape(row_count, model_width).astype(jnp.float32)
    normed = norm_rows(residual, gain_attn).astype(jnp.bfloat16)
    qkv_rows = product(normed, qkv_flat).reshape(row_count, 3, head_cols)
    query_raw = qkv_rows[:, 0].reshape(row_count, local_heads, head_size)
    key_raw = qkv_rows[:, 1].reshape(row_count, local_heads, head_size)
    queries = (
        norm_rows(query_raw, qk_gain[0])
        .astype(jnp.bfloat16)
        .reshape(slot_count, half_rows, head_cols)
    )
    keys_here = (
        norm_rows(key_raw, qk_gain[1])
        .astype(jnp.bfloat16)
        .reshape(slot_count, half_rows, head_cols)
    )
    values_here = qkv_rows[:, 2].astype(jnp.bfloat16).reshape(slot_count, half_rows, head_cols)
    bias_here = lax.dynamic_slice_in_dim(forget_bias, tensor_place * local_heads, local_heads)
    forget_pre = (product(normed, forget_full) + bias_here).reshape(
        slot_count, half_rows, local_heads
    )
    cum_here = jnp.cumsum(jax.nn.log_sigmoid(forget_pre), axis=1)
    keys_left, values_left = shifted((keys_here, values_here), "ctx", 1)
    cum_left = shifted(cum_here, "ctx", 1)
    cum_query = cum_here + cum_left[:, -1:, :]

    def by_head(values):
        shaped = values.reshape(slot_count, half_rows, local_heads, head_size)
        return jnp.transpose(shaped, (0, 2, 1, 3)).reshape(item_count, half_rows, head_size)

    def by_head_cum(values):
        return jnp.transpose(values, (0, 2, 1)).reshape(item_count, half_rows)

    def to_slots(values):
        shaped = values.reshape(slot_count, local_heads, half_rows, head_size)
        return jnp.transpose(shaped, (0, 2, 1, 3)).reshape(slot_count, half_rows, head_cols)

    def to_slots_cum(values):
        return jnp.transpose(values.reshape(slot_count, local_heads, half_rows), (0, 2, 1))

    q_items = by_head(queries)
    k_items = jnp.concatenate([by_head(keys_left), by_head(keys_here)], axis=1)
    v_items = jnp.concatenate([by_head(values_left), by_head(values_here)], axis=1)
    cq_items = by_head_cum(cum_query)
    ck_items = jnp.concatenate([by_head_cum(cum_left), cq_items], axis=1)
    place_ids = jnp.arange(half_rows, dtype=jnp.int32)
    earlier = jnp.broadcast_to(span_index > 0, (half_rows, half_rows))
    allowed = jnp.concatenate([earlier, place_ids[None, :] <= place_ids[:, None]], axis=1)

    def score_block(query_block, key_block, cum_rows, cum_cols):
        score_raw = (
            product_t(query_block, key_block) * score_scale + cum_rows[:, None] - cum_cols[None, :]
        )
        return jnp.where(allowed, score_raw, -jnp.inf)

    def forward_item(pieces):
        query_block, key_block, value_block, cum_rows, cum_cols = pieces
        score_vals = score_block(query_block, key_block, cum_rows, cum_cols)
        row_max = jnp.max(score_vals, axis=1, keepdims=True)
        expo = jnp.exp(score_vals - row_max)
        row_total = jnp.sum(expo, axis=1, keepdims=True)
        attn_probs = (expo / row_total).astype(jnp.bfloat16)
        return (product(attn_probs, value_block), (row_max + jnp.log(row_total))[:, 0])

    attended_items, lse_items = lax.map(
        forward_item, (q_items, k_items, v_items, cq_items, ck_items)
    )
    attended_rows = to_slots(attended_items).reshape(row_count, head_cols)
    opener = jax.nn.sigmoid(product(normed, ogate_full))
    gated = (attended_rows * opener).astype(jnp.bfloat16)
    branch_part = product_t(gated, out_full)
    branch_full = lax.psum(branch_part, "tp")
    middle = residual + branch_full
    middle_share = own_slice(middle)
    normed_mid = norm_rows(middle, gain_mlp).astype(jnp.bfloat16)
    both = product(normed_mid, gu_flat).reshape(row_count, 2, hidden_units)
    gate_pre = both[:, 0]
    up_pre = both[:, 1]
    gate_sig = jax.nn.sigmoid(gate_pre)
    hidden = (gate_pre * gate_sig * up_pre).astype(jnp.bfloat16)
    down_share = lax.psum_scatter(
        product_t(hidden, down_full)
        .reshape(slot_count, half_rows, model_width)
        .astype(jnp.bfloat16),
        "tp",
        scatter_dimension=1,
        tiled=True,
    ).astype(jnp.float32)
    output = (valid_own * (middle_share + down_share)).astype(jnp.bfloat16)
    cot_rows = full_cot.reshape(row_count, model_width) * valid_rows.astype(jnp.bfloat16)
    d_hidden = product(cot_rows, down_full)
    d_gate = d_hidden * up_pre * gate_sig * (1.0 + gate_pre * (1.0 - gate_sig))
    d_up = d_hidden * gate_pre * gate_sig
    d_both = (
        jnp.stack([d_gate, d_up], axis=1).astype(jnp.bfloat16).reshape(row_count, 2 * hidden_units)
    )
    grad_down = outer_rows(cot_rows, hidden)
    grad_gu = outer_rows(normed_mid, d_both).reshape(model_width, 2, hidden_units)
    d_mid_terms = product_t(d_both, gu_flat)
    d_normed_mid = lax.psum(d_mid_terms, "tp")
    _, pull_mid = jax.vjp(norm_rows, middle, gain_mlp)
    d_middle_norm, d_gain_mlp_all = pull_mid(d_normed_mid)
    d_middle = d_middle_norm + cot_rows.astype(jnp.float32)
    feat_share = model_width // tensor_size
    owner = jnp.arange(model_width, dtype=jnp.int32) // feat_share == tensor_place
    d_gain_mlp_own = jnp.where(owner, d_gain_mlp_all, 0.0)
    d_branch = d_middle.astype(jnp.bfloat16)
    d_middle_share = own_slice(d_middle)
    d_gated = product(d_branch, out_full)
    grad_out = outer_rows(d_branch, gated)
    d_attended = (d_gated * opener).astype(jnp.bfloat16)
    d_open = (d_gated * attended_rows * opener * (1.0 - opener)).astype(jnp.bfloat16)
    grad_ogate = outer_rows(normed, d_open)
    da_items = by_head(d_attended.reshape(slot_count, half_rows, head_cols))

    def backward_item(pieces):
        query_block, key_block, value_block, cum_rows, cum_cols, lse_block, grad_block = pieces
        score_vals = score_block(query_block, key_block, cum_rows, cum_cols)
        attn_probs = jnp.exp(score_vals - lse_block[:, None])
        d_probs = product_t(grad_block, value_block)
        centre = jnp.sum(attn_probs * d_probs, axis=1, keepdims=True)
        d_scores = (attn_probs * (d_probs - centre)).astype(jnp.bfloat16)
        d_query_block = product(d_scores, key_block) * score_scale
        d_key_block = outer_rows(d_scores, query_block) * score_scale
        d_value_block = outer_rows(attn_probs.astype(jnp.bfloat16), grad_block)
        d_cum_rows = jnp.sum(d_scores, axis=1, dtype=jnp.float32)
        d_cum_cols = -jnp.sum(d_scores, axis=0, dtype=jnp.float32)
        return (d_query_block, d_key_block, d_value_block, d_cum_rows, d_cum_cols)

    dq_items, dk_items, dv_items, dcq_items, dck_items = lax.map(
        backward_item, (q_items, k_items, v_items, cq_items, ck_items, lse_items, da_items)
    )
    dc_own = dcq_items + dck_items[:, half_rows:]
    dc_left = dck_items[:, :half_rows]
    dc_left = dc_left.at[:, -1].add(jnp.sum(dc_own, axis=1))
    back_keys, back_values, back_cum = (
        shifted(to_slots(dk_items[:, :half_rows]).astype(jnp.bfloat16), "ctx", -1).astype(
            jnp.float32
        ),
        shifted(to_slots(dv_items[:, :half_rows]).astype(jnp.bfloat16), "ctx", -1).astype(
            jnp.float32
        ),
        shifted(to_slots_cum(dc_left).astype(jnp.bfloat16), "ctx", -1).astype(jnp.float32),
    )
    d_query = to_slots(dq_items).reshape(row_count, local_heads, head_size)
    d_key = (to_slots(dk_items[:, half_rows:]) + back_keys).reshape(
        row_count, local_heads, head_size
    )
    d_value = (to_slots(dv_items[:, half_rows:]) + back_values).reshape(row_count, head_cols)
    d_cum = to_slots_cum(dc_own) + back_cum
    d_log = jnp.flip(jnp.cumsum(jnp.flip(d_cum, 1), axis=1), 1)
    d_forget = d_log * jax.nn.sigmoid(-forget_pre)
    d_bias_own = jnp.sum(d_forget, axis=(0, 1))
    d_forget_low = d_forget.reshape(row_count, local_heads).astype(jnp.bfloat16)
    grad_forget = outer_rows(normed, d_forget_low)
    _, pull_query = jax.vjp(norm_rows, query_raw, qk_gain[0])
    d_query_raw, d_query_gain = pull_query(d_query)
    _, pull_key = jax.vjp(norm_rows, key_raw, qk_gain[1])
    d_key_raw, d_key_gain = pull_key(d_key)
    d_mixed = (
        jnp.stack(
            [
                d_query_raw.reshape(row_count, head_cols),
                d_key_raw.reshape(row_count, head_cols),
                d_value,
            ],
            axis=1,
        )
        .astype(jnp.bfloat16)
        .reshape(row_count, 3 * head_cols)
    )
    grad_qkv = outer_rows(normed, d_mixed).reshape(model_width, 3, head_cols)
    d_normed = (
        product_t(d_mixed, qkv_flat)
        + product_t(d_open, ogate_full)
        + product_t(d_forget_low, forget_full)
    )
    root = lax.rsqrt(jnp.mean(residual * residual, axis=1, keepdims=True) + epsilon)
    unit = residual * root
    d_unit = d_normed * gain_attn
    dot_part = (jnp.sum(d_unit * unit, axis=1) / model_width).reshape(slot_count, half_rows)
    d_unit_share, dot_full = (
        lax.psum_scatter(
            d_unit.reshape(slot_count, half_rows, model_width).astype(jnp.bfloat16),
            "tp",
            scatter_dimension=1,
            tiled=True,
        ).astype(jnp.float32),
        lax.psum_scatter(
            dot_part.astype(jnp.bfloat16), "tp", scatter_dimension=1, tiled=True
        ).astype(jnp.float32),
    )
    unit_share = own_slice(unit)
    root_share = own_slice(root)
    input_grad = (
        d_middle_share + root_share * (d_unit_share - unit_share * dot_full[:, :, None])
    ).astype(jnp.bfloat16)
    grad_parts = (
        lax.psum_scatter(
            grad_qkv.astype(jnp.bfloat16), ("shard", "ctx"), scatter_dimension=0, tiled=True
        ).astype(jnp.float32),
        lax.psum_scatter(
            grad_forget.astype(jnp.bfloat16), ("shard", "ctx"), scatter_dimension=0, tiled=True
        ).astype(jnp.float32),
        lax.psum_scatter(
            grad_ogate.astype(jnp.bfloat16), ("shard", "ctx"), scatter_dimension=0, tiled=True
        ).astype(jnp.float32),
        lax.psum_scatter(
            grad_out.astype(jnp.bfloat16), ("shard", "ctx"), scatter_dimension=0, tiled=True
        ).astype(jnp.float32),
        lax.psum_scatter(
            grad_gu.astype(jnp.bfloat16), ("shard", "ctx"), scatter_dimension=0, tiled=True
        ).astype(jnp.float32),
        lax.psum_scatter(
            grad_down.astype(jnp.bfloat16), ("shard", "ctx"), scatter_dimension=0, tiled=True
        ).astype(jnp.float32),
    )
    bias_full = lax.dynamic_update_slice_in_dim(
        jnp.zeros(forget_bias.shape, jnp.float32), d_bias_own, tensor_place * local_heads, 0
    )
    gain_attn_part = jnp.sum(d_normed * unit, axis=0)
    small_parts = lax.psum(
        (gain_attn_part, d_gain_mlp_own, jnp.stack([d_query_gain, d_key_gain]), bias_full),
        ("shard", "ctx", "tp"),
    )
    return (
        output,
        input_grad,
        grad_parts[0],
        grad_parts[1],
        small_parts[3],
        grad_parts[2],
        grad_parts[3],
        grad_parts[4],
        grad_parts[5],
        small_parts[0],
        small_parts[1],
        small_parts[2],
    )


def solution(mesh):
    return jax.shard_map(
        body,
        mesh=mesh,
        in_specs=(
            P("shard", ("ctx", "tp"), None),
            P("shard", ("ctx", "tp"), None),
            P("shard"),
            P(("shard", "ctx"), None, "tp"),
            P(("shard", "ctx"), "tp"),
            P(),
            P(("shard", "ctx"), "tp"),
            P(("shard", "ctx"), "tp"),
            P(("shard", "ctx"), None, "tp"),
            P(("shard", "ctx"), "tp"),
            P(),
            P(),
            P(),
        ),
        out_specs=(
            P("shard", ("ctx", "tp"), None),
            P("shard", ("ctx", "tp"), None),
            P(("shard", "ctx"), None, "tp"),
            P(("shard", "ctx"), "tp"),
            P(),
            P(("shard", "ctx"), "tp"),
            P(("shard", "ctx"), "tp"),
            P(("shard", "ctx"), None, "tp"),
            P(("shard", "ctx"), "tp"),
            P(),
            P(),
            P(),
        ),
        check_vma=False,
    )
```

profile of v0, /device:TPU:0, one launch (start us, length us, event | category | flops | bytes accessed | tf_op | source)
XLA Modules:
  0.0 1049.7 jit_solution(11627350117377922482)
XLA Ops:
  11.9 10.6 %all-gather = bf16[8,192,6]{1,2,0:T(8,128)(2,1)S(1)} all-gather(bf16[1,192,6]{1,2,0:T(8,128)(2,1)} %bitcast.510), channel_id=1, replica_groups=mesh['shard'=4,'ctx'=2,'tp'=4] {'shard','ctx'}, dimensions={0}, use_global_device_ids=true | all-gather | bytes 20736 | tf_op jit(solution)/shard_map/all_gather | solution.py:70
  24.6 24.8 %all-gather.9.cloned.1.call-done = bf16[1,512,1536]{2,1,0:T(8,128)(2,1)} async-done(((bf16[1,128,1536]{2,1,0:T(8,128)(2,1)}), bf16[1,512,1536]{2,1,0:T(8,128)(2,1)}) %all-gather.9.cloned.1.call-update) | async-done | bytes 1572880 | tf_op jit(solution)/shard_map/all_gather | solution.py:65
  59.5 24.7 %all-gather.11.cloned.1.call-done = bf16[1536,3,384]{2,0,1:T(8,128)(2,1)} async-done(((bf16[192,3,384]{2,0,1:T(8,128)(2,1)}), bf16[1536,3,384]{2,0,1:T(8,128)(2,1)}) %all-gather.11.cloned.1.call-update) | async-done | bytes 3538960 | tf_op jit(solution)/shard_map/all_gather | solution.py:69
  84.2 6.1 copy.92
  118.7 37.0 %while.31 = (s32[]{:T(128)}, f32[6,512,64]{1,2,0:T(8,128)}, f32[6,512]{1,0:T(8,128)S(1)}, bf16[6,512,64]{2,1,0:T(8,128)(2,1)}, bf16[6,1024,64]{2,1,0:T(8,128)(2,...) while((s32[]{:T(128)}, f32[6,512,64]{1,2,0:T(8,128)}, ...), condition=%wide.region_8.9_spmd, body=%wide.region_5.8_spmd.sunk | while | flops 139460096 | bytes 7643265 | solution.py:151
  168.9 116.0 %all-reduce.5.cloned.1.call-done = f32[512,1536]{1,0:T(8,128)} async-done(((f32[512,1536]{1,0:T(8,128)}), f32[512,1536]{1,0:T(8,128)}) %all-reduce.5.cloned.1.call-update) | async-done | bytes 3145744 | tf_op jit(solution)/shard_map/psum | solution.py:158
  289.3 42.5 %all-gather.17.cloned.1.call-done = bf16[1536,2,1024]{2,0,1:T(8,128)(2,1)} async-done(((bf16[192,2,1024]{2,0,1:T(8,128)(2,1)}), bf16[1536,2,1024]{2,0,1:T(8,128)(2,1)}) %all-gather.17.cloned.1.call-update) | async-done | bytes 6291472 | tf_op jit(solution)/shard_map/all_gather | solution.py:73
  331.8 8.7 copy.104
  340.5 8.1 fusion.36
  348.6 21.9 %all-gather.21.cloned.1.call-done = bf16[1,512,1536]{2,1,0:T(8,128)(2,1)} async-done(((bf16[1,128,1536]{2,1,0:T(8,128)(2,1)}), bf16[1,512,1536]{2,1,0:T(8,128)(2,1)}) %all-gather.21.cloned.1.call-update) | async-done | bytes 1572880 | tf_op jit(solution)/shard_map/all_gather | solution.py:66
  370.5 33.1 %all-gather.19.cloned.1.call-done = bf16[1536,1024]{1,0:T(8,128)(2,1)} async-done(((bf16[192,1024]{1,0:T(8,128)(2,1)}), bf16[1536,1024]{1,0:T(8,128)(2,1)}) %all-gather.19.cloned.1.call-update) | async-done | bytes 3145744 | tf_op jit(solution)/shard_map/all_gather | solution.py:74
  410.9 8.0 convolution_bitcast_fusion.2
  423.5 6.7 fusion.47
  430.5 109.7 %all-reduce.7.cloned.1.call-done = f32[512,1536]{1,0:T(8,128)} async-done(((f32[512,1536]{1,0:T(8,128)}), f32[512,1536]{1,0:T(8,128)}) %all-reduce.7.cloned.1.call-update) | async-done | bytes 3145744 | tf_op jit(solution)/shard_map/psum | solution.py:186
  552.2 97.2 %while.32 = (s32[]{:T(128)}, f32[6,512,64]{1,2,0:T(8,128)}, f32[6,1024,64]{1,2,0:T(8,128)}, f32[6,1024,64]{1,2,0:T(8,128)}, f32[6,512]{1,0:T(8,128)}, /*index=5*...) while((s32[]{:T(128)}, f32[6,512,64]{1,2,0:T(8,128)}, ...), condition=%wide.region_18.19_spmd, body=%wide.region_14.18_spmd.sunk | while | flops 342981632 | bytes 20376776 | solution.py:216
  715.7 6.4 convolution_convert_fusion.2
  742.0 8.9 convolution_convert_fusion
  755.5 41.1 %all-reduce.1 = (f32[24]{0:T(128)}, f32[1536]{0:T(1024)}, f32[1536]{0:T(1024)}, f32[2,64]{1,0:T(2,128)}) all-reduce(f32[24]{0:T(128)S(1)} %dynamic_update_slice.28, f32[1536]{0:T(1024)S(1)} %get-tuple-element.207, f32[1536]{0:T(1024)S(1)} %fusion.108, ...), channel_id=1, replica_groups=mesh['shard'=4,'ctx'=2,'tp'=4] {'shard','ctx','tp'}, use_global_device_ids=true, to_apply=%region_30.31 | all-reduce | flops 3224 | bytes 25792 | tf_op jit(solution)/shard_map/psum | solution.py:308
  797.5 8.2 reduce-scatter.26.cloned.1.call-done
  807.7 37.9 %reduce-scatter.20.cloned.1.call-done = bf16[192,384]{1,0:T(8,128)(2,1)} async-done(((bf16[1536,384]{1,0:T(8,128)(2,1)}), bf16[192,384]{1,0:T(8,128)(2,1)}) %reduce-scatter.20.cloned.1.call-update) | async-done | bytes 147472 | tf_op jit(solution)/shard_map/reduce_scatter | solution.py:291
  847.2 38.6 %reduce-scatter.22.cloned.1.call-done = bf16[192,384]{1,0:T(8,128)(2,1)} async-done(((bf16[1536,384]{1,0:T(8,128)(2,1)}), bf16[192,384]{1,0:T(8,128)(2,1)}) %reduce-scatter.22.cloned.1.call-update) | async-done | bytes 147472 | tf_op jit(solution)/shard_map/reduce_scatter | solution.py:294
  887.5 36.4 %reduce-scatter.16.cloned.1.call-done = bf16[1,128,1536]{2,1,0:T(8,128)(2,1)} async-done(((bf16[1,512,1536]{2,1,0:T(8,128)(2,1)}), bf16[1,128,1536]{2,1,0:T(8,128)(2,1)}) %reduce-scatter.16.cloned.1.call-update) | async-done | bytes 393232 | tf_op jit(solution)/shard_map/reduce_scatter | solution.py:269
  926.1 48.2 %reduce-scatter.18.cloned.1.call-done = bf16[192,3,384]{2,0,1:T(8,128)(2,1)} async-done(((bf16[1536,3,384]{2,0,1:T(8,128)(2,1)}), bf16[192,3,384]{2,0,1:T(8,128)(2,1)}) %reduce-scatter.18.cloned.1.call-update) | async-done | bytes 442384 | tf_op jit(solution)/shard_map/reduce_scatter | solution.py:285
  976.3 63.0 %reduce-scatter.24.cloned.1.call-done = bf16[192,2,1024]{2,0,1:T(8,128)(2,1)} async-done(((bf16[1536,2,1024]{2,0,1:T(8,128)(2,1)}), bf16[192,2,1024]{2,0,1:T(8,128)(2,1)}) %reduce-scatter.24.cloned.1.call-update) | async-done | bytes 786448 | tf_op jit(solution)/shard_map/reduce_scatter | solution.py:297
  (443 shorter events, 323.4 us)
Async XLA Ops:
  7.2 42.2 %all-gather.9.cloned.1.call-start = ((), (), s32[]{:S(2)}) async-start(), calls=%async_computation.9 | async-start | bytes 1966080 | tf_op jit(solution)/shard_map/all_gather | solution.py:65
  7.9 76.3 %all-gather.11.cloned.1.call-start = ((), (), s32[]{:S(2)}) async-start(), calls=%async_computation.10 | async-start | bytes 3981312 | tf_op jit(solution)/shard_map/all_gather | solution.py:69
  8.7 147.0 %all-gather.13.cloned.1.call-start = ((), (), s32[]{:S(2)}) async-start(), calls=%async_computation.11 | async-start | bytes 1327104 | tf_op jit(solution)/shard_map/all_gather | solution.py:71
  9.4 150.3 %all-gather.15.cloned.1.call-start = ((), (), s32[]{:S(2)}) async-start(), calls=%async_computation.12 | async-start | bytes 1327104 | tf_op jit(solution)/shard_map/all_gather | solution.py:72
  10.0 274.9 %all-reduce.5.cloned.1.call-start = ((), (), s32[]{:S(2)}) async-start(), calls=%async_computation.13 | async-start | bytes 6291456 | tf_op jit(solution)/shard_map/psum | solution.py:158
  55.5 2.4 collective-permute-start.1
  96.7 13.4 %collective-permute-start = (bf16[1,512,384]{1,2,0:T(8,128)(2,1)}, bf16[1,512,384]{1,2,0:T(8,128)(2,1)}, u32[]{:S(2)}, u32[]{:S(2)}) collective-permute-start(bf16[1,512,384]{1,2,0:T(8,128)(2,1)} %multiply_convert_fusion.9), channel_id=1, source_target_pairs={{0,4},{1,5},{2,6},{3,7},{8,12},{9,13},{10,14},{11,15},{16,20},{17,... | collective-permute-start | bytes 1179656 | tf_op jit(solution)/shard_map/ppermute | solution.py:13
  99.6 12.7 %collective-permute-start.2 = (bf16[1,512,384]{1,2,0:T(8,128)(2,1)}, bf16[1,512,384]{1,2,0:T(8,128)(2,1)}, u32[]{:S(2)}, u32[]{:S(2)}) collective-permute-start(bf16[1,512,384]{1,2,0:T(8,128)(2,1)} %slice_bitcast_fusion.5), channel_id=1, source_target_pairs={{0,4},{1,5},{2,6},{3,7},{8,12},{9,13},{10,14},{11,15},{16,20},{17,... | collective-permute-start | bytes 1179656 | tf_op jit(solution)/shard_map/ppermute | solution.py:13
  163.7 168.1 %all-gather.17.cloned.1.call-start = ((), (), s32[]{:S(2)}) async-start(), calls=%async_computation.14 | async-start | bytes 7077888 | tf_op jit(solution)/shard_map/all_gather | solution.py:73
  165.9 204.6 %all-gather.21.cloned.1.call-start = ((), (), s32[]{:S(2)}) async-start(), calls=%async_computation.17 | async-start | bytes 1966080 | tf_op jit(solution)/shard_map/all_gather | solution.py:66
  166.7 236.9 %all-gather.19.cloned.1.call-start = ((), (), s32[]{:S(2)}) async-start(), calls=%async_computation.15 | async-start | bytes 3538944 | tf_op jit(solution)/shard_map/all_gather | solution.py:74
  167.4 372.7 %all-reduce.7.cloned.1.call-start = ((), (), s32[]{:S(2)}) async-start(), calls=%async_computation.18 | async-start | bytes 6291456 | tf_op jit(solution)/shard_map/psum | solution.py:186
  418.9 332.6 %reduce-scatter.14.cloned.1.call-start = ((), (), s32[]{:S(2)}) async-start(), calls=%async_computation.16 | async-start | bytes 1966080 | tf_op jit(solution)/shard_map/reduce_scatter | solution.py:167
  430.2 323.7 %reduce-scatter.30.cloned.1.call-start = ((), (), s32[]{:S(2)}) async-start(), calls=%async_computation.26 | async-start | bytes 442368
  653.4 51.8 %collective-permute-start.4 = (bf16[1,512,384]{1,2,0:T(8,128)(2,1)}, bf16[1,512,384]{1,2,0:T(8,128)(2,1)}, u32[]{:S(2)}, u32[]{:S(2)}) collective-permute-start(bf16[1,512,384]{1,2,0:T(8,128)(2,1)} %bitcast.100), channel_id=1, source_target_pairs={{4,0},{5,1},{6,2},{7,3},{12,8},{13,9},{14,10},{15,11},{20,16},{21,... | collective-permute-start | bytes 1179656 | tf_op jit(solution)/shard_map/ppermute | solution.py:13
  656.6 44.0 %collective-permute-start.3 = (bf16[1,512,384]{1,2,0:T(8,128)(2,1)}, bf16[1,512,384]{1,2,0:T(8,128)(2,1)}, u32[]{:S(2)}, u32[]{:S(2)}) collective-permute-start(bf16[1,512,384]{1,2,0:T(8,128)(2,1)} %bitcast.90), channel_id=1, source_target_pairs={{4,0},{5,1},{6,2},{7,3},{12,8},{13,9},{14,10},{15,11},{20,16},{21,... | collective-permute-start | bytes 1179656 | tf_op jit(solution)/shard_map/ppermute | solution.py:13
  665.8 6.0 collective-permute-start.5
  700.3 96.4 %reduce-scatter.28.cloned.1.call-start = ((), (), s32[]{:S(2)}) async-start(), calls=%async_computation.25 | async-start | bytes 163840
  715.7 90.0 %reduce-scatter.26.cloned.1.call-start = ((), (), s32[]{:S(2)}) async-start(), calls=%async_computation.24 | async-start | bytes 3538944 | tf_op jit(solution)/shard_map/reduce_scatter | solution.py:300
  722.2 123.4 %reduce-scatter.20.cloned.1.call-start = ((), (), s32[]{:S(2)}) async-start(), calls=%async_computation.21 | async-start | bytes 1327104 | tf_op jit(solution)/shard_map/reduce_scatter | solution.py:291
  725.9 159.9 %reduce-scatter.22.cloned.1.call-start = ((), (), s32[]{:S(2)}) async-start(), calls=%async_computation.22 | async-start | bytes 1327104 | tf_op jit(solution)/shard_map/reduce_scatter | solution.py:294
  728.0 195.8 %reduce-scatter.16.cloned.1.call-start = ((), (), s32[]{:S(2)}) async-start(), calls=%async_computation.19 | async-start | bytes 1966080 | tf_op jit(solution)/shard_map/reduce_scatter | solution.py:269
  728.6 245.7 %reduce-scatter.18.cloned.1.call-start = ((), (), s32[]{:S(2)}) async-start(), calls=%async_computation.20 | async-start | bytes 3981312 | tf_op jit(solution)/shard_map/reduce_scatter | solution.py:285
  734.9 304.4 %reduce-scatter.24.cloned.1.call-start = ((), (), s32[]{:S(2)}) async-start(), calls=%async_computation.23 | async-start | bytes 7077888 | tf_op jit(solution)/shard_map/reduce_scatter | solution.py:297
  (75 other events, 701.1 us)
Sparse Core Ops, SparseCore 0:
  9.6 39.7 all-gather.8
  51.3 32.8 all-gather.10
  86.1 24.0 all-gather.12
  112.0 24.0 all-gather.14
  163.8 121.0 all-reduce.4
  287.2 44.5 all-gather.16
  333.4 37.0 all-gather.20
  372.4 31.1 all-gather.18
  419.0 121.0 all-reduce.6
  542.3 34.2 reduce-scatter.13
  700.4 35.1 reduce-scatter.29
  738.2 19.1 reduce-scatter.27
  761.2 44.4 reduce-scatter.25
  808.8 36.7 reduce-scatter.19
  849.0 36.7 reduce-scatter.21
  888.6 35.2 reduce-scatter.15
  927.2 47.0 reduce-scatter.17
  977.5 61.7 reduce-scatter.23
where the time goes:
time: 1060 us; the launch traced here: 1050 us
  waiting for transfers between devices  611 us (58%)
  matrix products  162 us (15%)
  local copies, waits for them, and re-layouts  121 us (11%)
  other arithmetic  75.4 us (7%)
  blocking collectives  51.8 us (5%)
  between operations  16.4 us (2%)
  starting transfers between devices  12.2 us (1%)
    psum x1, waiting for transfers between devices, body(): branch_full = lax.psum(branch_part, 'tp')  116 us
    psum x1, waiting for transfers between devices, body(): d_normed_mid = lax.psum(d_mid_terms, 'tp')  110 us
    reduce_scatter x1, waiting for transfers between devices, body(): lax.psum_scatter(grad_gu.astype(jnp.bfloat16), ('shard', 'ctx'), scatter_...  63 us
    dot_general x24, matrix products, product_t(): lax.dot_general(left, right, (((1,), (1,)), ((), ())), preferred_element_...  58 us
    dot_general x18, matrix products, outer_rows(): lax.dot_general(left, right, (((0,), (0,)), ((), ())), preferred_element_...  52.8 us
    dot_general x18, matrix products, product(): return jnp.dot(left, right, preferred_element_type=jnp.float32)  51.2 us
    reduce_scatter x1, waiting for transfers between devices, body(): lax.psum_scatter(grad_qkv.astype(jnp.bfloat16), ('shard', 'ctx'), scatter...  48.2 us
    all_gather x1, waiting for transfers between devices, body(): lax.all_gather(w_gu, ('shard', 'ctx'), axis=0, tiled=True)  42.5 us
  transfers between devices with their start and end apart: 24, of which 14 were waited for; matrix products, arithmetic and copies ran while one was open for 31% of the time, Pallas kernels for 0%

commit v1 on v0

--- a/solution.py
+++ b/solution.py
@@ -155,7 +155,7 @@
     opener = jax.nn.sigmoid(product(normed, ogate_full))
     gated = (attended_rows * opener).astype(jnp.bfloat16)
     branch_part = product_t(gated, out_full)
-    branch_full = lax.psum(branch_part, "tp")
+    branch_full = jnp.sum(lax.all_gather(branch_part, "tp"), axis=0)
     middle = residual + branch_full
     middle_share = own_slice(middle)
     normed_mid = norm_rows(middle, gain_mlp).astype(jnp.bfloat16)

time: 1060 us -> 1130 us (1.066)
  waiting for transfers between devices: 611 us -> 672 us
    all_gather x0 -> x1, waiting for transfers between devices: none -> 211 us  [body(): branch_full = jnp.sum(lax.all_gather(branch_part, 'tp'), axis=0)]
    psum x1 -> x0, waiting for transfers between devices: 116 us -> none  [body(): branch_full = lax.psum(branch_part, 'tp')]
    all_gather x1, waiting for transfers between devices: 42.5 us -> 16.1 us  [body(): lax.all_gather(w_gu, ('shard', 'ctx'), axis=0, tiled=True)]
    unnamed x149 -> x159, local copies, waits for them, and re-layouts: 20.5 us -> 25.2 us
  transfers between devices with their start and end apart: 24 -> 24, of which waited for: 14 -> 14; matrix products, arithmetic and copies ran while one was open for 31% -> 30% of each run, Pallas kernels for 0% -> 0%
where the time goes in v1:
time: 1130 us; the launch traced here: 1120 us
  waiting for transfers between devices  672 us (59%)
  matrix products  158 us (14%)
  local copies, waits for them, and re-layouts  125 us (11%)
  other arithmetic  83.3 us (7%)
  blocking collectives  51.7 us (5%)
  between operations  16.1 us (1%)
  starting transfers between devices  12.2 us (1%)
    all_gather x1, waiting for transfers between devices, body(): branch_full = jnp.sum(lax.all_gather(branch_part, 'tp'), axis=0)  211 us
    psum x1, waiting for transfers between devices, body(): d_normed_mid = lax.psum(d_mid_terms, 'tp')  110 us
    reduce_scatter x1, waiting for transfers between devices, body(): lax.psum_scatter(grad_gu.astype(jnp.bfloat16), ('shard', 'ctx'), scatter_...  63 us
    dot_general x24, matrix products, product_t(): lax.dot_general(left, right, (((1,), (1,)), ((), ())), preferred_element_...  58 us
    dot_general x18, matrix products, outer_rows(): lax.dot_general(left, right, (((0,), (0,)), ((), ())), preferred_element_...  52.1 us
    reduce_scatter x1, waiting for transfers between devices, body(): lax.psum_scatter(grad_qkv.astype(jnp.bfloat16), ('shard', 'ctx'), scatter...  48.3 us
    dot_general x18, matrix products, product(): return jnp.dot(left, right, preferred_element_type=jnp.float32)  48.2 us
    psum x1, blocking collectives, body(): lax.psum((gain_attn_part, d_gain_mlp_own, jnp.stack([d_query_gain, d_key_...  41.1 us
  transfers between devices with their start and end apart: 24, of which 14 were waited for; matrix products, arithmetic and copies ran while one was open for 30% of the time, Pallas kernels for 0%

profile of v1, /device:TPU:0, one launch (start us, length us, event | category | flops | bytes accessed | tf_op | source)
XLA Modules:
  0.0 1119.1 jit_solution(10644206559586680112)
XLA Ops:
  13.5 10.5 all-gather.1
  26.1 23.3 %all-gather.11.cloned.1.call-done = bf16[1,512,1536]{2,1,0:T(8,128)(2,1)} async-done(((bf16[1,128,1536]{2,1,0:T(8,128)(2,1)}), bf16[1,512,1536]{2,1,0:T(8,128)(2,1)}) %all-gather.11.cloned.1.call-update) | async-done | bytes 1572880 | tf_op jit(solution)/shard_map/all_gather | solution.py:65
  59.5 24.7 %all-gather.13.cloned.1.call-done = bf16[1536,3,384]{2,0,1:T(8,128)(2,1)} async-done(((bf16[192,3,384]{2,0,1:T(8,128)(2,1)}), bf16[1536,3,384]{2,0,1:T(8,128)(2,1)}) %all-gather.13.cloned.1.call-update) | async-done | bytes 3538960 | tf_op jit(solution)/shard_map/all_gather | solution.py:69
  84.2 6.1 copy.92
  119.4 37.0 %while.31 = (s32[]{:T(128)}, f32[6,512,64]{1,2,0:T(8,128)}, f32[6,512]{1,0:T(8,128)S(1)}, bf16[6,512,64]{2,1,0:T(8,128)(2,1)}, bf16[6,1024,64]{2,1,0:T(8,128)(2,...) while((s32[]{:T(128)}, f32[6,512,64]{1,2,0:T(8,128)}, ...), condition=%wide.region_8.9_spmd, body=%wide.region_5.8_spmd.sunk | while | flops 139460096 | bytes 7643265 | solution.py:151
  167.3 16.1 %all-gather.19.cloned.1.call-done = bf16[1536,2,1024]{2,0,1:T(8,128)(2,1)} async-done(((bf16[192,2,1024]{2,0,1:T(8,128)(2,1)}), bf16[1536,2,1024]{2,0,1:T(8,128)(2,1)}) %all-gather.19.cloned.1.call-update) | async-done | bytes 6291472 | tf_op jit(solution)/shard_map/all_gather | solution.py:73
  183.4 8.7 copy.104
  192.1 211.0 %all-gather.25.cloned.1.call-done = f32[2048,1536]{1,0:T(8,128)} async-done(((f32[512,1536]{1,0:T(8,128)}), f32[2048,1536]{1,0:T(8,128)}) %all-gather.25.cloned.1.call-update) | async-done | bytes 12582928 | tf_op jit(solution)/shard_map/all_gather | solution.py:158
  403.0 8.0 reduce_sum.192
  424.1 15.9 %all-gather.23.cloned.1.call-done = bf16[1,512,1536]{2,1,0:T(8,128)(2,1)} async-done(((bf16[1,128,1536]{2,1,0:T(8,128)(2,1)}), bf16[1,512,1536]{2,1,0:T(8,128)(2,1)}) %all-gather.23.cloned.1.call-update) | async-done | bytes 1572880 | tf_op jit(solution)/shard_map/all_gather | solution.py:66
  439.9 33.1 %all-gather.21.cloned.1.call-done = bf16[1536,1024]{1,0:T(8,128)(2,1)} async-done(((bf16[192,1024]{1,0:T(8,128)(2,1)}), bf16[1536,1024]{1,0:T(8,128)(2,1)}) %all-gather.21.cloned.1.call-update) | async-done | bytes 3145744 | tf_op jit(solution)/shard_map/all_gather | solution.py:74
  480.3 8.0 convolution_bitcast_fusion.2
  493.1 6.6 fusion.50
  500.0 109.6 %all-reduce.4.cloned.1.call-done = f32[512,1536]{1,0:T(8,128)} async-done(((f32[512,1536]{1,0:T(8,128)}), f32[512,1536]{1,0:T(8,128)}) %all-reduce.4.cloned.1.call-update) | async-done | bytes 3145744 | tf_op jit(solution)/shard_map/psum | solution.py:186
  621.7 97.3 %while.32 = (s32[]{:T(128)}, f32[6,512,64]{1,2,0:T(8,128)}, f32[6,1024,64]{1,2,0:T(8,128)}, f32[6,1024,64]{1,2,0:T(8,128)}, f32[6,512]{1,0:T(8,128)}, /*index=5*...) while((s32[]{:T(128)}, f32[6,512,64]{1,2,0:T(8,128)}, ...), condition=%wide.region_18.19_spmd, body=%wide.region_14.18_spmd.sunk | while | flops 342981632 | bytes 20376776 | solution.py:216
  785.5 6.3 convolution_convert_fusion.2
  811.6 8.2 convolution_convert_fusion
  824.5 41.1 %all-reduce.1 = (f32[24]{0:T(128)}, f32[1536]{0:T(1024)}, f32[1536]{0:T(1024)}, f32[2,64]{1,0:T(2,128)}) all-reduce(f32[24]{0:T(128)S(1)} %dynamic_update_slice.28, f32[1536]{0:T(1024)S(1)} %get-tuple-element.207, f32[1536]{0:T(1024)S(1)} %fusion.109, ...), channel_id=1, replica_groups=mesh['shard'=4,'ctx'=2,'tp'=4] {'shard','ctx','tp'}, use_global_device_ids=true, to_apply=%region_30.31 | all-reduce | flops 3224 | bytes 25792 | tf_op jit(solution)/shard_map/psum | solution.py:308
  866.5 8.9 reduce-scatter.26.cloned.1.call-done
  877.4 37.9 %reduce-scatter.20.cloned.1.call-done = bf16[192,384]{1,0:T(8,128)(2,1)} async-done(((bf16[1536,384]{1,0:T(8,128)(2,1)}), bf16[192,384]{1,0:T(8,128)(2,1)}) %reduce-scatter.20.cloned.1.call-update) | async-done | bytes 147472 | tf_op jit(solution)/shard_map/reduce_scatter | solution.py:291
  917.0 38.6 %reduce-scatter.22.cloned.1.call-done = bf16[192,384]{1,0:T(8,128)(2,1)} async-done(((bf16[1536,384]{1,0:T(8,128)(2,1)}), bf16[192,384]{1,0:T(8,128)(2,1)}) %reduce-scatter.22.cloned.1.call-update) | async-done | bytes 147472 | tf_op jit(solution)/shard_map/reduce_scatter | solution.py:294
  957.2 36.4 %reduce-scatter.16.cloned.1.call-done = bf16[1,128,1536]{2,1,0:T(8,128)(2,1)} async-done(((bf16[1,512,1536]{2,1,0:T(8,128)(2,1)}), bf16[1,128,1536]{2,1,0:T(8,128)(2,1)}) %reduce-scatter.16.cloned.1.call-update) | async-done | bytes 393232 | tf_op jit(solution)/shard_map/reduce_scatter | solution.py:269
  995.8 48.3 %reduce-scatter.18.cloned.1.call-done = bf16[192,3,384]{2,0,1:T(8,128)(2,1)} async-done(((bf16[1536,3,384]{2,0,1:T(8,128)(2,1)}), bf16[192,3,384]{2,0,1:T(8,128)(2,1)}) %reduce-scatter.18.cloned.1.call-update) | async-done | bytes 442384 | tf_op jit(solution)/shard_map/reduce_scatter | solution.py:285
  1046.0 63.0 %reduce-scatter.24.cloned.1.call-done = bf16[192,2,1024]{2,0,1:T(8,128)(2,1)} async-done(((bf16[1536,2,1024]{2,0,1:T(8,128)(2,1)}), bf16[192,2,1024]{2,0,1:T(8,128)(2,1)}) %reduce-scatter.24.cloned.1.call-update) | async-done | bytes 786448 | tf_op jit(solution)/shard_map/reduce_scatter | solution.py:297
  (455 shorter events, 332.3 us)
Async XLA Ops:
  7.2 42.2 %all-gather.11.cloned.1.call-start = ((), (), s32[]{:S(2)}) async-start(), calls=%async_computation.9 | async-start | bytes 1966080 | tf_op jit(solution)/shard_map/all_gather | solution.py:65
  7.9 76.3 %all-gather.13.cloned.1.call-start = ((), (), s32[]{:S(2)}) async-start(), calls=%async_computation.10 | async-start | bytes 3981312 | tf_op jit(solution)/shard_map/all_gather | solution.py:69
  8.7 147.7 %all-gather.15.cloned.1.call-start = ((), (), s32[]{:S(2)}) async-start(), calls=%async_computation.11 | async-start | bytes 1327104 | tf_op jit(solution)/shard_map/all_gather | solution.py:71
  9.4 151.0 %all-gather.17.cloned.1.call-start = ((), (), s32[]{:S(2)}) async-start(), calls=%async_computation.12 | async-start | bytes 1327104 | tf_op jit(solution)/shard_map/all_gather | solution.py:72
  10.0 173.4 %all-gather.19.cloned.1.call-start = ((), (), s32[]{:S(2)}) async-start(), calls=%async_computation.13 | async-start | bytes 7077888 | tf_op jit(solution)/shard_map/all_gather | solution.py:73
  12.3 390.7 %all-gather.25.cloned.1.call-start = ((), (), s32[]{:S(2)}) async-start(), calls=%async_computation.24 | async-start | bytes 15728640 | tf_op jit(solution)/shard_map/all_gather | solution.py:158
  55.6 2.4 collective-permute-start.1
  96.0 14.8 %collective-permute-start = (bf16[1,512,384]{1,2,0:T(8,128)(2,1)}, bf16[1,512,384]{1,2,0:T(8,128)(2,1)}, u32[]{:S(2)}, u32[]{:S(2)}) collective-permute-start(bf16[1,512,384]{1,2,0:T(8,128)(2,1)} %multiply_convert_fusion.8), channel_id=1, source_target_pairs={{0,4},{1,5},{2,6},{3,7},{8,12},{9,13},{10,14},{11,15},{16,20},{17,... | collective-permute-start | bytes 1179656 | tf_op jit(solution)/shard_map/ppermute | solution.py:13
  99.7 13.3 %collective-permute-start.2 = (bf16[1,512,384]{1,2,0:T(8,128)(2,1)}, bf16[1,512,384]{1,2,0:T(8,128)(2,1)}, u32[]{:S(2)}, u32[]{:S(2)}) collective-permute-start(bf16[1,512,384]{1,2,0:T(8,128)(2,1)} %slice_bitcast_fusion.5), channel_id=1, source_target_pairs={{0,4},{1,5},{2,6},{3,7},{8,12},{9,13},{10,14},{11,15},{16,20},{17,... | collective-permute-start | bytes 1179656 | tf_op jit(solution)/shard_map/ppermute | solution.py:13
  164.4 275.6 %all-gather.23.cloned.1.call-start = ((), (), s32[]{:S(2)}) async-start(), calls=%async_computation.16 | async-start | bytes 1966080 | tf_op jit(solution)/shard_map/all_gather | solution.py:66
  165.1 307.9 %all-gather.21.cloned.1.call-start = ((), (), s32[]{:S(2)}) async-start(), calls=%async_computation.14 | async-start | bytes 3538944 | tf_op jit(solution)/shard_map/all_gather | solution.py:74
  165.9 443.7 %all-reduce.4.cloned.1.call-start = ((), (), s32[]{:S(2)}) async-start(), calls=%async_computation.17 | async-start | bytes 6291456 | tf_op jit(solution)/shard_map/psum | solution.py:186
  488.4 332.2 %reduce-scatter.14.cloned.1.call-start = ((), (), s32[]{:S(2)}) async-start(), calls=%async_computation.15 | async-start | bytes 1966080 | tf_op jit(solution)/shard_map/reduce_scatter | solution.py:167
  499.7 323.2 %reduce-scatter.30.cloned.1.call-start = ((), (), s32[]{:S(2)}) async-start(), calls=%async_computation.26 | async-start | bytes 442368
  723.0 51.9 %collective-permute-start.4 = (bf16[1,512,384]{1,2,0:T(8,128)(2,1)}, bf16[1,512,384]{1,2,0:T(8,128)(2,1)}, u32[]{:S(2)}, u32[]{:S(2)}) collective-permute-start(bf16[1,512,384]{1,2,0:T(8,128)(2,1)} %bitcast.103), channel_id=1, source_target_pairs={{4,0},{5,1},{6,2},{7,3},{12,8},{13,9},{14,10},{15,11},{20,16},{21,... | collective-permute-start | bytes 1179656 | tf_op jit(solution)/shard_map/ppermute | solution.py:13
  726.2 44.0 %collective-permute-start.3 = (bf16[1,512,384]{1,2,0:T(8,128)(2,1)}, bf16[1,512,384]{1,2,0:T(8,128)(2,1)}, u32[]{:S(2)}, u32[]{:S(2)}) collective-permute-start(bf16[1,512,384]{1,2,0:T(8,128)(2,1)} %bitcast.93), channel_id=1, source_target_pairs={{4,0},{5,1},{6,2},{7,3},{12,8},{13,9},{14,10},{15,11},{20,16},{21,... | collective-permute-start | bytes 1179656 | tf_op jit(solution)/shard_map/ppermute | solution.py:13
  735.4 6.0 collective-permute-start.5
  769.8 95.9 %reduce-scatter.28.cloned.1.call-start = ((), (), s32[]{:S(2)}) async-start(), calls=%async_computation.25 | async-start | bytes 163840
  785.4 90.0 %reduce-scatter.26.cloned.1.call-start = ((), (), s32[]{:S(2)}) async-start(), calls=%async_computation.23 | async-start | bytes 3538944 | tf_op jit(solution)/shard_map/reduce_scatter | solution.py:300
  791.8 123.5 %reduce-scatter.20.cloned.1.call-start = ((), (), s32[]{:S(2)}) async-start(), calls=%async_computation.20 | async-start | bytes 1327104 | tf_op jit(solution)/shard_map/reduce_scatter | solution.py:291
  795.5 160.0 %reduce-scatter.22.cloned.1.call-start = ((), (), s32[]{:S(2)}) async-start(), calls=%async_computation.21 | async-start | bytes 1327104 | tf_op jit(solution)/shard_map/reduce_scatter | solution.py:294
  797.7 195.9 %reduce-scatter.16.cloned.1.call-start = ((), (), s32[]{:S(2)}) async-start(), calls=%async_computation.18 | async-start | bytes 1966080 | tf_op jit(solution)/shard_map/reduce_scatter | solution.py:269
  798.3 245.8 %reduce-scatter.18.cloned.1.call-start = ((), (), s32[]{:S(2)}) async-start(), calls=%async_computation.19 | async-start | bytes 3981312 | tf_op jit(solution)/shard_map/reduce_scatter | solution.py:285
  804.5 304.5 %reduce-scatter.24.cloned.1.call-start = ((), (), s32[]{:S(2)}) async-start(), calls=%async_computation.22 | async-start | bytes 7077888 | tf_op jit(solution)/shard_map/reduce_scatter | solution.py:297
  (80 other events, 654.8 us)
Sparse Core Ops, SparseCore 0:
  9.6 39.7 all-gather.10
  51.3 32.8 all-gather.12
  86.1 24.0 all-gather.14
  112.0 24.0 all-gather.16
  137.8 45.5 all-gather.18
  184.8 218.1 all-gather.24
  404.6 35.2 all-gather.22
  441.8 31.1 all-gather.20
  488.5 121.0 all-reduce.3
  611.7 34.2 reduce-scatter.13
  769.9 35.1 reduce-scatter.29
  807.8 19.1 reduce-scatter.27
  830.7 44.6 reduce-scatter.25
  878.5 36.7 reduce-scatter.19
  918.7 36.7 reduce-scatter.21
  958.3 35.2 reduce-scatter.15
  996.9 47.0 reduce-scatter.17
  1047.2 61.6 reduce-scatter.23
